TPU v7x, 32 devices: a whole 2x2x4 slice. The times are simulated.
32 devices in a mesh: groups: 2 (over y), tile: 4 (over z), vec: 4 (over x, core).
Axes of the slice: x: 2, y: 2, z: 4, core: 2. Of those that a mesh axis runs over, the one named last changes fastest.
Arguments:
- vectors: float32 [2, 256, 3, 8192], P(None, 'vec', None, ('groups', 'tile')), parts along dimension 3, may hold values from -6 to 6
- links: float32 [3, 2, 3, 3, 8192], P(None, None, None, None, ('groups', 'tile')), parts along dimension 4, may hold values from -2.5 to 2.5
- momenta: int32 [8, 3], replicated, may hold values from -2 to 2
- directions: int32 [2], replicated, may hold values from 0 to 5
Outputs:
- elementals: float32 [512, 2, 2, 8, 256], P(('groups', 'tile'), None, None, None, 'vec'), parts along dimension 0
There are 2 independent parts, one for each index of `groups`. A program takes and returns all parts, laid end to end along the dimension named above; an argument that names none is the same for every part. Nothing has to cross between parts.
Inputs may be any that keep to these rules, and one draw needn't show every extreme that they name: directions 0, 1, 2 step forward along the first, second, third dimension; 3, 4, 5 step backward along them.
All inputs are finite; a program needn't handle non-finite values.
Results may differ from a plain program's by a relative error of at most 0.00012.
Values sent between devices are 32-bit elements; how exact they have to be, the bound alone decides.
A program may use at most 128 MiB of HBM per device.

v0:
```python
import functools
import math

import jax
import jax.numpy as jnp
from jax import lax
from jax.experimental import pallas as pl
from jax.experimental.pallas import tpu as pltpu
from jax.sharding import PartitionSpec as P

LY = 16
LZ = 32
ITERS = 4
PLANE = LY * LZ
LANES = 128
PER_PLANE = PLANE // LANES
HOP_SCALE = 0.125
VMEM_LIMIT = 60 * 1024 * 1024
CORES = 2
MESH = pl.DeviceIdType.MESH


def lane_index(like):
    return lax.broadcasted_iota(jnp.int32, like.shape, len(like.shape) - 1)


def shift_z(value, step):
    axis = len(value.shape) - 1
    lane = lane_index(value) % LZ
    if step > 0:
        plain = pltpu.roll(value, LANES - 1, axis)
        wrapped = pltpu.roll(value, LZ - 1, axis)
        return jnp.where(lane == LZ - 1, wrapped, plain)
    plain = pltpu.roll(value, 1, axis)
    wrapped = pltpu.roll(value, LANES - LZ + 1, axis)
    return jnp.where(lane == 0, wrapped, plain)


def shift_y(value, other, step):
    axis = len(value.shape) - 1
    lane = lane_index(value)
    if step > 0:
        return pltpu.roll(jnp.where(lane < LZ, other, value), LANES - LZ, axis)
    return pltpu.roll(jnp.where(lane >= LANES - LZ, other, value), LZ, axis)


def in_plane(chunk, step):
    base = chunk // PER_PLANE * PER_PLANE
    return base + (chunk + step + PER_PLANE) % PER_PLANE


def link_row(links, chunk, spatial, part, row, column):
    index = (part * 3 + row) * 3 + column
    return links[chunk, spatial, index : index + 1, :]


def apply_link(links, chunk, spatial, dagger, field, total):
    for row in range(3):
        real, imag = total[row], total[3 + row]
        for column in range(3):
            a, b = (column, row) if dagger else (row, column)
            lr = link_row(links, chunk, spatial, 0, a, b)
            li = link_row(links, chunk, spatial, 1, a, b)
            vr, vi = field[column], field[3 + column]
            if dagger:
                dr = lr * vr + li * vi
                di = lr * vi - li * vr
            else:
                dr = lr * vr - li * vi
                di = lr * vi + li * vr
            real = dr if real is None else real + dr
            imag = di if imag is None else imag + di
        total[row], total[3 + row] = real, imag
    return total


def moved(read, chunk, spatial, step, ahead_x):
    if spatial == 0:
        return [read(ahead_x, comp) for comp in range(6)]
    if spatial == 1:
        other = in_plane(chunk, step)
        return [shift_y(read(chunk, comp), read(other, comp), step) for comp in range(6)]
    return [shift_z(read(chunk, comp), step) for comp in range(6)]


def remote(src, dst, send, recv, axis, device):
    return pltpu.make_async_remote_copy(
        src_ref=src,
        dst_ref=dst,
        send_sem=send,
        recv_sem=recv,
        device_id={axis: device},
        device_id_type=MESH,
    )


def greet(places):
    barrier = pltpu.get_barrier_semaphore()
    for axis, device in places:
        pl.semaphore_signal(barrier, inc=1, device_id={axis: device}, device_id_type=MESH)
    pl.semaphore_wait(barrier, len(places))


def spread_kernel(tiles, vecs, links_in, field_in, gathered, own_table, *scratch):
    field, first, second, pieces, links, back, *sems = scratch
    local_sem, link_z, link_x, link_p, link_f, out_sem, back_sem, x_sem, p_sem, f_sem = sems
    groups, every = field.shape[0], field.shape[1]
    chunks = every // tiles
    some = pieces.shape[2]
    me, vec = lax.axis_index("tile"), lax.axis_index("vec")
    partner = vec + 1 - 2 * (vec % CORES)
    others = vecs // CORES
    tile_at = lambda turn: (me + turn) % tiles
    vec_at = lambda turn: (vec + CORES * turn) % vecs
    slab = lambda tile: pl.ds(tile * chunks, chunks)

    greet(
        [("tile", tile_at(turn)) for turn in range(1, tiles)]
        + [("vec", vec_at(turn)) for turn in range(1, others)]
        + [("vec", partner)]
    )

    waits = []

    def begin(copy):
        copy.start()
        waits.append(copy)
        return copy

    own_links = pltpu.make_async_copy(links_in, pieces.at[me, vec], local_sem.at[0])
    own_links.start()
    links_z = [
        begin(remote(links_in, pieces.at[me, vec], link_z.at[0, turn], link_z.at[1, turn], "tile", tile_at(turn)))
        for turn in range(1, tiles)
    ]
    own_field, sent = [], []
    for group in range(groups):
        own_field.append(
            pltpu.make_async_copy(
                field_in.at[group, me], field.at[group, slab(me)], local_sem.at[1 + group]
            )
        )
        own_field[group].start()
        sent.append(
            [
                begin(
                    remote(
                        field_in.at[group, tile_at(turn)],
                        field.at[group, slab(me)],
                        out_sem.at[0, group, turn],
                        out_sem.at[1, group, turn],
                        "tile",
                        tile_at(turn),
                    )
                )
                for turn in range(1, tiles)
            ]
        )

    own_links.wait()
    for copy in links_z:
        copy.wait_recv()
    mine = pieces.at[:, vec]
    links_x = [
        begin(remote(mine, mine, link_x.at[0, turn], link_x.at[1, turn], "vec", vec_at(turn)))
        for turn in range(1, others)
    ]
    links_p = begin(remote(mine, mine, link_p.at[0], link_p.at[1], "vec", partner))
    links_f = []
    for turn in range(1, others):
        links_x[turn - 1].wait_recv()
        got = pieces.at[:, vec_at(others - turn)]
        links_f.append(
            begin(remote(got, got, link_f.at[0, turn], link_f.at[1, turn], "vec", partner))
        )
    links_p.wait_recv()
    for copy in links_f:
        copy.wait_recv()

    @pl.loop(0, every)
    def _(chunk):
        place = chunk % chunks
        links[chunk] = pieces[chunk // chunks, place // some, place % some]

    @pl.loop(0, every)
    def _(chunk):
        back[chunk, 0] = links[(chunk - PER_PLANE + every) % every, 0]
        back[chunk, 1] = shift_y(links[chunk, 1], links[in_plane(chunk, -1), 1], -1)
        back[chunk, 2] = shift_z(links[chunk, 2], -1)

    @pl.loop(0, chunks)
    def _(chunk):
        for spatial in range(3):
            at = me * chunks + chunk
            own_table[spatial, chunk] = links[at, spatial]
            for part in range(2):
                for row in range(3):
                    for column in range(3):
                        place = (part * 3 + row) * 3 + column
                        value = link_row(back, at, spatial, part, column, row)
                        own_table[3 + spatial, chunk, place : place + 1, :] = -value if part else value

    def hop(source, previous, target):
        @pl.loop(0, every)
        def _(chunk):
            read = lambda at, comp: source[at, comp]
            total = [None] * 6
            for spatial in range(3):
                ahead = moved(read, chunk, spatial, 1, (chunk + PER_PLANE) % every)
                total = apply_link(links, chunk, spatial, False, ahead, total)
                behind = moved(
                    read, chunk, spatial, -1, (chunk - PER_PLANE + every) % every
                )
                total = apply_link(back, chunk, spatial, True, behind, total)
            for comp in range(6):
                if previous is None:
                    target[chunk, comp] = HOP_SCALE * total[comp]
                else:
                    target[chunk, comp] = (
                        2.0 * HOP_SCALE * total[comp] - previous[chunk, comp]
                    )

    returned, across = {}, {}

    def share(group, turn):
        if turn > 0:
            returned[group, turn].wait_recv()
        else:
            returned[group, turn].wait()
        at = gathered.at[vec, tile_at(tiles - turn), group]
        for step in range(1, others):
            across[group, turn, step] = begin(
                remote(
                    at, at, x_sem.at[0, group, turn, step], x_sem.at[1, group, turn, step], "vec", vec_at(step)
                )
            )
        across[group, turn, 0] = begin(
            remote(at, at, p_sem.at[0, group, turn], p_sem.at[1, group, turn], "vec", partner)
        )

    forwards = []

    def forward(group, turn):
        for step in range(1, others):
            across[group, turn, step].wait_recv()
            at = gathered.at[vec_at(others - step), tile_at(tiles - turn), group]
            forwards.append(
                begin(
                    remote(
                        at, at, f_sem.at[0, group, turn, step], f_sem.at[1, group, turn, step], "vec", partner
                    )
                )
            )

    def steps_of(group):
        todo = [lambda: share(group, 0)]
        for turn in range(1, tiles):
            todo.append(lambda turn=turn: (share(group, turn), forward(group, turn - 1)))
        todo.append(lambda: forward(group, tiles - 1))
        return todo

    todo = []
    for group in range(groups):
        own_field[group].wait()
        for copy in sent[group]:
            copy.wait_recv()
        buffers = [field.at[group], first.at[group], second]
        hop(buffers[0], None, buffers[1])
        for order in range(1, ITERS):
            if order >= 2 and len(todo) > 0:
                todo.pop(0)()
            hop(buffers[1], buffers[0], buffers[2])
            buffers = [buffers[1], buffers[2], buffers[0]]
        done = buffers[1]
        returned[group, 0] = pltpu.make_async_copy(
            done.at[slab(me)], gathered.at[vec, me, group], local_sem.at[1 + groups + group]
        )
        returned[group, 0].start()
        for turn in range(1, tiles):
            returned[group, turn] = begin(
                remote(
                    done.at[slab(tile_at(turn))],
                    gathered.at[vec, me, group],
                    back_sem.at[0, group, turn],
                    back_sem.at[1, group, turn],
                    "tile",
                    tile_at(turn),
                )
            )
        todo += steps_of(group)
        todo.pop(0)()
    for step in todo:
        step()
    for group in range(groups):
        for turn in range(tiles):
            across[group, turn, 0].wait_recv()
    for copy in forwards:
        copy.wait_recv()
    for copy in waits:
        copy.wait_send()


def split(value):
    high = value.astype(jnp.bfloat16)
    low = (value - high.astype(jnp.float32)).astype(jnp.bfloat16)
    return high, low


def shifts(read, chunk):
    other = lambda step: in_plane(chunk, step)
    found = []
    for comp in range(6):
        here = read(chunk, comp)
        found.append(
            (
                read(chunk + PER_PLANE, comp),
                shift_y(here, read(other(1), comp), 1),
                shift_z(here, 1),
                read(chunk - PER_PLANE, comp),
                shift_y(here, read(other(-1), comp), -1),
                shift_z(here, -1),
            )
        )
    return found


def contract_kernel(
    tiles, dirs_ref, gathered, before, after, table, cos_ref, sin_ref, out_ref, *scratch
):
    cols, shifted, staged, rows, left_hi, left_lo, *scratch = scratch
    right_hi, right_lo, sums, part, got, load_sem, sum_sem = scratch[0:2], scratch[2:4], *scratch[4:]
    chunks, disps, columns = shifted.shape[0], shifted.shape[1], shifted.shape[3]
    vecs, tile_count, groups, size = staged.shape[1], staged.shape[2], staged.shape[3], staged.shape[5]
    row_count = left_hi.shape[1]
    share = row_count // tiles
    width, depth = right_hi[0].shape[1], right_hi[0].shape[2]
    span = depth // (3 * LANES)
    steps = chunks // span
    some = width // (disps * columns)
    blocks = part.shape[0]
    pieces = tile_count * groups
    me, vec = lax.axis_index("tile"), lax.axis_index("vec")

    def load(chunk):
        return pltpu.make_async_copy(
            gathered.at[:, :, :, chunk], staged.at[chunk % 2], load_sem.at[chunk % 2]
        )

    copies = [
        pltpu.make_async_copy(before, cols.at[:, :, 0:PER_PLANE], load_sem.at[2]),
        pltpu.make_async_copy(
            gathered.at[vec], cols.at[:, :, PER_PLANE : PER_PLANE + chunks], load_sem.at[3]
        ),
        pltpu.make_async_copy(
            after, cols.at[:, :, PER_PLANE + chunks : 2 * PER_PLANE + chunks], load_sem.at[4]
        ),
    ]
    for copy in copies:
        copy.start()
    load(0).start()
    up, down = jnp.minimum(me + 1, tiles - 1), jnp.maximum(me - 1, 0)
    greet([("tile", (me + turn) % tiles) for turn in range(1, tiles)])
    for copy in copies:
        copy.wait()

    unrolled = math.gcd(pieces, 4)

    @pl.loop(0, chunks * (pieces // unrolled))
    def _(index):
        chunk = index % chunks
        results = []
        for inner in range(unrolled):
            piece = index // chunks * unrolled + inner
            read = lambda where, comp, piece=piece: cols[
                piece // groups, piece % groups, where + PER_PLANE, comp
            ]
            found = shifts(read, chunk)
            home = pl.multiple_of(piece * size, size)
            for disp in range(disps):
                heading = dirs_ref[disp]
                source = []
                for comp in range(6):
                    value = found[comp][0]
                    for other in range(1, 6):
                        value = jnp.where(heading == other, found[comp][other], value)
                    source.append(value)
                for row in range(3):
                    real = imag = None
                    for column in range(3):
                        place = row * 3 + column
                        lr = table[heading, chunk, place : place + 1, :]
                        li = table[heading, chunk, 9 + place : 10 + place, :]
                        dr = lr * source[column] - li * source[3 + column]
                        di = lr * source[3 + column] + li * source[column]
                        real = dr if real is None else real + dr
                        imag = di if imag is None else imag + di
                    results.append((disp, row, home, real))
                    results.append((disp, 3 + row, home, imag))
        for disp, comp, home, value in results:
            shifted[chunk, disp, comp, pl.ds(home, size), :] = value

    @pl.loop(0, chunks)
    def _(chunk):
        @pl.when(chunk + 1 < chunks)
        def _():
            load(chunk + 1).start()

        load(chunk).wait()
        slot = chunk % 2
        if size % 8 == 0:
            flat = lambda comp: staged[slot, :, :, :, comp].reshape(row_count, LANES)
        else:
            for owner in range(vecs):
                for tile in range(tile_count):
                    for group in range(groups):
                        place = ((owner * tile_count + tile) * groups + group) * size
                        for comp in range(6):
                            rows[comp, place : place + size, :] = staged[
                                slot, owner, tile, group, comp
                            ]
            flat = lambda comp: rows[comp]
        for colour in range(3):
            at = pl.ds(pl.multiple_of((chunk * 3 + colour) * LANES, LANES), LANES)
            real, imag = flat(colour), flat(3 + colour)
            for kind, value in enumerate((real, imag, real + imag)):
                left_hi[kind, :, at], left_lo[kind, :, at] = split(value)

    dims = (((1,), (1,)), ((), ()))
    dot = functools.partial(
        lax.dot_general, dimension_numbers=dims, preferred_element_type=jnp.float32
    )

    def prepare(block, step, which):
        for inner in range(span):
            chunk = step * span + inner
            for p in range(some):
                c = cos_ref[chunk, pl.ds(block * some + p, 1), :]
                s = sin_ref[chunk, pl.ds(block * some + p, 1), :]
                for disp in range(disps):
                    place = (p * disps + disp) * columns
                    home = slice(place, place + columns)
                    for colour in range(3):
                        first = (inner * 3 + colour) * LANES
                        at = slice(first, first + LANES)
                        dr = shifted[chunk, disp, colour]
                        di = shifted[chunk, disp, 3 + colour]
                        real = c * dr + s * di
                        imag = c * di - s * dr
                        for kind, value in enumerate((real, imag, imag - real)):
                            high, low = split(value)
                            right_hi[which][kind, home, at] = high
                            right_lo[which][kind, home, at] = low

    def product(kind, step, which):
        at = slice(step * depth, (step + 1) * depth)
        high, low = left_hi[kind, :, at], left_lo[kind, :, at]
        right = right_hi[which][kind]
        return dot(high, right_lo[which][kind]) + dot(low, right) + dot(high, right)

    def parcel(block, target, device, way):
        return remote(
            part.at[block, target],
            got.at[way, block, target],
            sum_sem.at[way, 0, block, target],
            sum_sem.at[way, 1, block, target],
            "tile",
            device,
        )

    def serve(time):
        for way, (age, device) in enumerate(((me, up), (tiles - 1 - me, down))):
            block = time - age

            @pl.when((block >= 0) & (block < blocks))
            def _(way=way, age=age, device=device, block=block):
                for step in range(1, tiles):
                    target = tiles - step if way == 0 else step - 1

                    def receive(target=target):
                        parcel(block, target, device, way).wait_recv()
                        part[block, target] = part[block, target] + got[way, block, target]

                    ahead = me < target if way == 0 else me > target
                    pl.when(ahead & (age > 0))(receive)
                    pl.when(ahead)(lambda target=target: parcel(block, target, device, way).start())

    prepare(0, 0, 0)

    @pl.loop(0, blocks)
    def _(block):
        for step in range(steps):
            after_last = step + 1 == steps
            if steps % 2:
                prepare(block, step, step % 2)
            else:
                prepare(
                    jnp.minimum(block + 1, blocks - 1) if after_last else block,
                    0 if after_last else step + 1,
                    (step + 1) % 2,
                )
            for kind in range(3):
                value = product(kind, step, step % 2)
                sums[kind] = value if step == 0 else sums[kind] + value
        total = sums[0] + sums[1]
        both = sums[2] + sums[0] - sums[1]
        for tile in range(tiles):
            part[block, tile, 0] = total[tile * share : (tile + 1) * share]
            part[block, tile, 1] = both[tile * share : (tile + 1) * share]
        serve(block)

    @pl.loop(blocks, blocks + tiles - 1)
    def _(time):
        serve(time)

    for block in range(blocks):
        for way, (age, device) in enumerate(((me, up), (tiles - 1 - me, down))):

            @pl.when(age > 0)
            def _(way=way, device=device):
                parcel(block, me, device, way).wait_recv()
                part[block, me] = part[block, me] + got[way, block, me]

        for kind in range(2):
            out_ref[kind, :, block * width : (block + 1) * width] = part[block, me, kind]
        for target in range(tiles):
            pl.when(me < target)(lambda: parcel(block, target, up, 0).wait_send())
            pl.when(me > target)(lambda: parcel(block, target, down, 1).wait_send())


def phases(momenta, flat_index, extent_x):
    coord_x = flat_index // PLANE
    coord_y = flat_index % PLANE // LZ
    coord_z = flat_index % LZ
    part_x = jnp.mod(momenta[:, 0:1] * coord_x[None], extent_x).astype(jnp.float32) / extent_x
    part_y = jnp.mod(momenta[:, 1:2] * coord_y[None], LY).astype(jnp.float32) / LY
    part_z = jnp.mod(momenta[:, 2:3] * coord_z[None], LZ).astype(jnp.float32) / LZ
    angle = 2.0 * math.pi * (part_x + part_y + part_z)
    return (jnp.cos(angle), jnp.sin(angle))


def local(vectors, links, momenta, directions):
    nv = vectors.shape[1]
    sites = vectors.shape[3]
    tiles = lax.axis_size("tile")
    vecs = lax.axis_size("vec")
    disps = directions.shape[0]
    moms = momenta.shape[0]
    chunks = sites // LANES
    every = chunks * tiles
    share = nv // tiles
    norm = 1.0 / math.sqrt(3.0 * sites * tiles)
    me = lax.axis_index("tile")
    groups = 2 if share % 16 == 0 else 1
    size = share // groups
    some_chunks = chunks // vecs

    own_links = links.reshape(3, 18, chunks, LANES).transpose(2, 0, 1, 3)
    quarter = lax.dynamic_slice_in_dim(
        own_links, lax.axis_index("vec") * some_chunks, some_chunks, 0
    )
    field = vectors.reshape(2, tiles, groups, size, 3, chunks, LANES)
    field = field.transpose(2, 1, 5, 0, 4, 3, 6)
    field = field.reshape(groups, tiles, chunks, 6, size, LANES)

    vmem = pl.BlockSpec(memory_space=pltpu.VMEM)
    smem = pl.BlockSpec(memory_space=pltpu.SMEM)
    anywhere = pl.BlockSpec(memory_space=pl.ANY)
    f32 = lambda *shape: jax.ShapeDtypeStruct(shape, jnp.float32)
    room = lambda *shape: pltpu.VMEM(shape, jnp.float32)
    half = lambda *shape: pltpu.VMEM(shape, jnp.bfloat16)
    dma = lambda *shape: pltpu.SemaphoreType.DMA(shape)
    others = vecs // CORES
    gathered, table = pl.pallas_call(
        functools.partial(spread_kernel, tiles, vecs),
        out_shape=(
            f32(vecs, tiles, groups, chunks, 6, size, LANES),
            f32(6, chunks, 18, LANES),
        ),
        in_specs=[anywhere, anywhere],
        out_specs=(anywhere, vmem),
        scratch_shapes=[
            room(groups, every, 6, size, LANES),
            room(groups, every, 6, size, LANES),
            room(every, 6, size, LANES),
            room(tiles, vecs, some_chunks, 3, 18, LANES),
            room(every, 3, 18, LANES),
            room(every, 3, 18, LANES),
            dma(1 + 2 * groups),
            dma(2, tiles),
            dma(2, max(others, 1)),
            dma(2),
            dma(2, max(others, 1)),
            dma(2, groups, tiles),
            dma(2, groups, tiles),
            dma(2, groups, tiles, max(others, 1)),
            dma(2, groups, tiles),
            dma(2, groups, tiles, max(others, 1)),
        ],
        compiler_params=pltpu.CompilerParams(
            vmem_limit_bytes=VMEM_LIMIT, collective_id=0, has_side_effects=True
        ),
        name="spread",
    )(quarter, field)

    def passed(value, steps):
        return lax.ppermute(value, "tile", [(i, (i + steps) % tiles) for i in range(tiles)])

    def halo(heading, steps, first):
        def fetch(value):
            own = lax.dynamic_index_in_dim(value, lax.axis_index("vec"), 0, False)
            return passed(own[:, :, first : first + PER_PLANE], steps)

        def nothing(value):
            return jnp.zeros((tiles, groups, PER_PLANE, 6, size, LANES), jnp.float32)

        return lax.cond(jnp.any(directions == heading), fetch, nothing, gathered)

    before = halo(3, 1, chunks - PER_PLANE)
    after = halo(0, -1, 0)

    flat_index = me * sites + jnp.arange(sites, dtype=jnp.int32)
    cosine, sine = phases(momenta, flat_index, sites * tiles // PLANE)
    cosine = (cosine * norm).reshape(moms, chunks, LANES).transpose(1, 0, 2)
    sine = (sine * norm).reshape(moms, chunks, LANES).transpose(1, 0, 2)

    row_count = nv * vecs
    some = max(1, min(moms, 256 // (disps * nv)))
    blocks = moms // some
    width = some * disps * nv
    depth = 3 * sites
    span = 2 if chunks % 4 == 0 else chunks
    right = half(3, width, 3 * span * LANES)
    mine = pl.pallas_call(
        functools.partial(contract_kernel, tiles),
        out_shape=f32(2, row_count // tiles, moms * disps * nv),
        in_specs=[smem, anywhere, anywhere, anywhere, vmem, vmem, vmem],
        out_specs=vmem,
        scratch_shapes=[
            room(tiles, groups, chunks + 2 * PER_PLANE, 6, size, LANES),
            room(chunks, disps, 6, nv, LANES),
            room(2, vecs, tiles, groups, 6, size, LANES),
            room(6, row_count, LANES) if size % 8 else room(1, 8, LANES),
            half(3, row_count, depth),
            half(3, row_count, depth),
            right,
            right,
            right,
            right,
            room(3, row_count, width),
            room(blocks, tiles, 2, row_count // tiles, width),
            room(2, blocks, tiles, 2, row_count // tiles, width),
            dma(5),
            dma(2, 2, blocks, tiles),
        ],
        compiler_params=pltpu.CompilerParams(
            vmem_limit_bytes=VMEM_LIMIT, collective_id=1, has_side_effects=True
        ),
        name="contract",
    )(directions, gathered, before, after, table, cosine, sine)
    mine = mine.reshape(2, row_count // tiles, moms, disps, nv)
    return mine.transpose(1, 3, 0, 2, 4)


def solution(mesh):
    return jax.shard_map(
        local,
        mesh=mesh,
        in_specs=(
            P(None, "vec", None, ("groups", "tile")),
            P(None, None, None, None, ("groups", "tile")),
            P(),
            P(),
        ),
        out_specs=P(("groups", "tile"), None, None, None, "vec"),
        check_vma=False,
    )
```

profile of v0, /device:TPU:0, one launch (start us, length us, event | category | flops | bytes accessed | tf_op | source)
XLA Modules:
  0.0 180.0 jit_solution(14131149612898448057)
XLA Ops:
  0.0 1.1 copy.7
  1.1 0.1 reshape.134
  1.2 0.6 copy.15
  1.9 2.7 %copy.9 = f32[2,4,2,8,3,8,128]{6,3,4,0,5,1,2:T(8,128)} copy(f32[2,4,2,8,3,8,128]{6,3,5,2,1,4,0:T(8,128)} %bitcast.21) | data formatting | bytes 3145728 | tf_op jit(solution)/shard_map/reshape | solution.py:561
  4.6 0.0 copy-start.1
  4.6 101.4 %spread.1 = (f32[4,4,2,8,6,8,128]{6,5,4,3,2,1,0:T(8,128)}, f32[6,8,18,128]{3,2,1,0:T(8,128)}) custom-call(f32[2,3,18,128]{3,2,1,0:T(8,128)} %bitcast.22, f32[2,4,8,6,8,128]{5,4,3,2,1,0:T(8,128)} %bitcast.20), custom_call_target="tpu_custom_call" | custom-call | tf_op jit(solution)/shard_map/spread/pallas_call | solution.py:573
  106.0 0.0 copy-done.1
  106.0 0.7 compare_reduce_fusion
  107.4 1.0 conditional.2
  107.4 0.9 broadcast.258
  109.0 0.0 copy-start
  109.0 0.9 conditional.3
  109.0 0.9 broadcast.259
  110.0 0.0 copy-done
  110.0 0.9 sine_multiply_fusion
  110.9 66.2 %contract.1 = f32[2,64,1024]{2,1,0:T(8,128)} custom-call(s32[2]{0:T(128)} %dirs_ref.1, f32[4,4,2,8,6,8,128]{6,5,4,3,2,1,0:T(8,128)} %get-tuple-element.15.gathered, f32[4,2,4,6,8,128]{5,4,3,2,1,0:T(8,128)} %get-tuple-element.26.before, f32[4,2,4,6,8,128]{5,4,3,2,1,0:T(8,128)} %get-tuple-element.27.after, f32[6,8,18,128]{3,2,1,0:T(8,128)} %get-tuple-element.16.table, ...), custom_call_target="tpu_custom_call" | custom-call | tf_op jit(solution)/shard_map/contract/pallas_call | solution.py:633
  177.1 1.8 reshape.137
  178.9 1.1 copy.14
  (4 shorter events, 0.1 us)
Async XLA Ops:
  4.6 101.4 %copy-start.1 = (s32[2]{0:T(128)S(1)}, s32[2]{0:T(128)}, u32[]{:S(2)}) copy-start(s32[2]{0:T(128)} %dirs_ref.1) | copy-start | bytes 28
  109.0 1.0 copy-start
where the time goes:
time: 180 us
  Pallas kernels  168 us (93%)
  local copies, waits for them, and re-layouts  9.34 us (5%)
    pallas_call x1, Pallas kernels, local(): pl.pallas_call(functools.partial(spread_kernel, tiles, vecs), out_shape=(...  101 us
    pallas_call x1, Pallas kernels, local(): pl.pallas_call(functools.partial(contract_kernel, tiles), out_shape=f32(2...  66.2 us

commit v1 on v0

--- a/solution.py
+++ b/solution.py
@@ -200,25 +200,29 @@
                         value = link_row(back, at, spatial, part, column, row)
                         own_table[3 + spatial, chunk, place : place + 1, :] = -value if part else value
 
+    pair = math.gcd(every, 2)
+
     def hop(source, previous, target):
-        @pl.loop(0, every)
-        def _(chunk):
+        @pl.loop(0, every // pair)
+        def _(index):
             read = lambda at, comp: source[at, comp]
-            total = [None] * 6
-            for spatial in range(3):
-                ahead = moved(read, chunk, spatial, 1, (chunk + PER_PLANE) % every)
-                total = apply_link(links, chunk, spatial, False, ahead, total)
-                behind = moved(
-                    read, chunk, spatial, -1, (chunk - PER_PLANE + every) % every
-                )
-                total = apply_link(back, chunk, spatial, True, behind, total)
-            for comp in range(6):
-                if previous is None:
-                    target[chunk, comp] = HOP_SCALE * total[comp]
-                else:
-                    target[chunk, comp] = (
-                        2.0 * HOP_SCALE * total[comp] - previous[chunk, comp]
+            for inner in range(pair):
+                chunk = index * pair + inner
+                total = [None] * 6
+                for spatial in range(3):
+                    ahead = moved(read, chunk, spatial, 1, (chunk + PER_PLANE) % every)
+                    total = apply_link(links, chunk, spatial, False, ahead, total)
+                    behind = moved(
+                        read, chunk, spatial, -1, (chunk - PER_PLANE + every) % every
                     )
+                    total = apply_link(back, chunk, spatial, True, behind, total)
+                for comp in range(6):
+                    if previous is None:
+                        target[chunk, comp] = HOP_SCALE * total[comp]
+                    else:
+                        target[chunk, comp] = (
+                            2.0 * HOP_SCALE * total[comp] - previous[chunk, comp]
+                        )
 
     returned, across = {}, {}
 

time: 180 us -> 171 us (0.950)
  Pallas kernels: 168 us -> 158 us
    pallas_call x1, Pallas kernels: 101 us -> 92.9 us  [local(): pl.pallas_call(functools.partial(spread_kernel, tiles, vecs), out_shape=(...]
where the time goes in v1:
time: 171 us; the launch traced here: 170 us
  Pallas kernels  158 us (92%)
  local copies, waits for them, and re-layouts  9.34 us (5%)
    pallas_call x1, Pallas kernels, local(): pl.pallas_call(functools.partial(spread_kernel, tiles, vecs), out_shape=(...  92.9 us
    pallas_call x1, Pallas kernels, local(): pl.pallas_call(functools.partial(contract_kernel, tiles), out_shape=f32(2...  65.2 us

profile of v1, /device:TPU:0, one launch (start us, length us, event | category | flops | bytes accessed | tf_op | source)
XLA Modules:
  0.0 170.4 jit_solution(8827268684687633566)
XLA Ops:
  0.0 1.1 copy.7
  1.1 0.1 reshape.134
  1.2 0.6 copy.15
  1.9 2.7 %copy.9 = f32[2,4,2,8,3,8,128]{6,3,4,0,5,1,2:T(8,128)} copy(f32[2,4,2,8,3,8,128]{6,3,5,2,1,4,0:T(8,128)} %bitcast.21) | data formatting | bytes 3145728 | tf_op jit(solution)/shard_map/reshape | solution.py:565
  4.6 0.0 copy-start.1
  4.6 92.9 %spread.1 = (f32[4,4,2,8,6,8,128]{6,5,4,3,2,1,0:T(8,128)}, f32[6,8,18,128]{3,2,1,0:T(8,128)}) custom-call(f32[2,3,18,128]{3,2,1,0:T(8,128)} %bitcast.22, f32[2,4,8,6,8,128]{5,4,3,2,1,0:T(8,128)} %bitcast.20), custom_call_target="tpu_custom_call" | custom-call | tf_op jit(solution)/shard_map/spread/pallas_call | solution.py:577
  97.4 0.0 copy-done.1
  97.4 0.7 compare_reduce_fusion
  98.8 1.0 conditional.2
  98.8 0.9 broadcast.258
  100.4 0.0 copy-start
  100.4 0.9 conditional.3
  100.5 0.9 broadcast.259
  101.4 0.0 copy-done
  101.5 0.9 sine_multiply_fusion
  102.3 65.2 %contract.1 = f32[2,64,1024]{2,1,0:T(8,128)} custom-call(s32[2]{0:T(128)} %dirs_ref.1, f32[4,4,2,8,6,8,128]{6,5,4,3,2,1,0:T(8,128)} %get-tuple-element.15.gathered, f32[4,2,4,6,8,128]{5,4,3,2,1,0:T(8,128)} %get-tuple-element.26.before, f32[4,2,4,6,8,128]{5,4,3,2,1,0:T(8,128)} %get-tuple-element.27.after, f32[6,8,18,128]{3,2,1,0:T(8,128)} %get-tuple-element.16.table, ...), custom_call_target="tpu_custom_call" | custom-call | tf_op jit(solution)/shard_map/contract/pallas_call | solution.py:637
  167.5 1.8 %reshape.137 = f32[2,64,8,2,64]{4,3,2,1,0:T(2,128)S(1)} reshape(f32[2,64,1024]{2,1,0:T(8,128)} %contract.1) | data formatting | bytes 1048576 | tf_op jit(solution)/shard_map/reshape | solution.py:664
  169.3 1.1 copy.14
  (4 shorter events, 0.1 us)
Async XLA Ops:
  4.6 92.9 %copy-start.1 = (s32[2]{0:T(128)S(1)}, s32[2]{0:T(128)}, u32[]{:S(2)}) copy-start(s32[2]{0:T(128)} %dirs_ref.1) | copy-start | bytes 28
  100.4 1.0 copy-start
